TPU v7x, 256 devices: a whole 4x4x8 slice. The times are simulated.
256 devices in a mesh: grp: 8 (over x, core), seq: 32 (over z, y).
Axes of the slice: x: 4, y: 4, z: 8, core: 2. Of those that a mesh axis runs over, the one named last changes fastest.
Arguments:
- queries: bfloat16 [8, 3, 32, 128, 512], P('grp', None, 'seq'), may hold values from -120 to 120
- key_input: bfloat16 [8, 3, 32, 128, 512], P('grp', None, 'seq'), may hold values from -8 to 8
- value_input: bfloat16 [8, 3, 32, 128, 512], P('grp', None, 'seq'), may hold values from -6 to 6
- grad_output: bfloat16 [8, 3, 32, 128, 512], P('grp', None, 'seq'), may hold values from -6 to 6
- block_lists: int32 [768, 16], replicated, may hold values from -1 to 767, as said below
- block_flags: int32 [768, 16], replicated, may hold values from 0 to 1, as said below
Outputs:
- attended: bfloat16 [8, 3, 32, 128, 512], P('grp', None, 'seq')
- grad_queries: bfloat16 [8, 3, 32, 128, 512], P('grp', None, 'seq')
- grad_keys: bfloat16 [8, 3, 32, 128, 512], P('grp', None, 'seq')
- grad_values: bfloat16 [8, 3, 32, 128, 512], P('grp', None, 'seq')
Inputs may be any that keep to these rules, and one draw needn't show every extreme that they name: `block_lists`: entry 0 of row t is t itself; the other used entries of a row are distinct tiles u < t, each either in the same block of 96 tiles as t, or in an earlier block with u % 32 == t % 32; used entries come first and -1 fills the rest. The 3 rows t = (a * 3 + b) * 32 + c that share a and c name together at most one tile of the form (a2 * 3 + b2) * 32 + c2 for each pair (a2, c2) other than (a, c). block_flags[t, 0] is 1 for every t; a flag whose list entry is -1 has no effect.
All inputs are finite; a program needn't handle non-finite values.
Results may differ from a plain program's by a relative error of at most 0.029.
Values may be sent and summed in bfloat16 or wider, within the bound.
No kernel may reach another device: no remote copies, remote signals or barrier semaphores. Data moves between devices by JAX's collectives and lax.ppermute only.
A program may use at most 256 MiB of HBM per device.

v0:
```python
import jax
import jax.numpy as jnp
from jax import lax
from jax.sharding import PartitionSpec as P

HEADS = 8
HEAD_DIM = 64
floor_score = -1e30


def locate(entry_ids, group_tiles, columns):
    safe_ids = jnp.maximum(entry_ids, 0)
    within = safe_ids % group_tiles
    return (safe_ids // group_tiles, within // columns, within % columns)


def per_device(queries, key_input, value_input, grad_output, block_lists, block_flags):
    tile_dev = queries.shape[1]
    tile_rows = queries.shape[3]
    width = queries.shape[4]
    entries = block_lists.shape[1]
    columns = lax.axis_size("seq")
    groups = lax.axis_size("grp")
    group_at = lax.axis_index("grp")
    column_at = lax.axis_index("seq")
    group_tiles = tile_dev * columns
    query_tiles = queries.reshape(tile_dev, tile_rows, width)
    key_tiles = key_input.reshape(tile_dev, tile_rows, width)
    value_tiles = value_input.reshape(tile_dev, tile_rows, width)
    grad_tiles = grad_output.reshape(tile_dev, tile_rows, width)
    ranks = jnp.arange(tile_dev, dtype=jnp.int32)
    column_ids = jnp.arange(columns, dtype=jnp.int32)
    group_ids = jnp.arange(groups, dtype=jnp.int32)
    my_tiles = (group_at * tile_dev + ranks) * columns + column_at
    my_lists = jnp.take(block_lists, my_tiles, axis=0)
    my_flags = jnp.take(block_flags, my_tiles, axis=0)
    present = my_lists >= 0
    owner_group, owner_rank, owner_column = locate(my_lists, group_tiles, columns)
    same_group = owner_group == group_at
    is_own = present & same_group & (owner_column == column_at)
    is_near = present & same_group & (owner_column != column_at)
    is_far = present & jnp.logical_not(same_group)
    group_rows = lax.dynamic_slice_in_dim(block_lists, group_at * group_tiles, group_tiles, 0)
    group_rows = group_rows.reshape(tile_dev, columns, entries)
    row_group, row_rank, row_column = locate(group_rows, group_tiles, columns)
    named_here = (group_rows >= 0) & (row_group == group_at) & (row_column == column_at)
    near_rank = jnp.max(jnp.where(named_here, row_rank, -1), axis=(0, 2))
    near_rank = jnp.where(column_ids == column_at, -1, near_rank)
    column_rows = jnp.take(
        block_lists.reshape(groups, tile_dev, columns, entries), column_at, axis=2
    )
    far_group, far_rank_all, far_column = locate(column_rows, group_tiles, columns)
    named_far = (column_rows >= 0) & (far_group == group_at) & (far_column == column_at)
    far_rank = jnp.max(jnp.where(named_far, far_rank_all, -1), axis=(1, 2))
    far_rank = jnp.where(group_ids == group_at, -1, far_rank)
    wanted = jnp.max(
        jnp.where(
            is_near[:, :, None] & (owner_column[:, :, None] == column_ids),
            owner_rank[:, :, None],
            -1,
        ),
        axis=(0, 1),
    )
    pieces = (
        lax.all_gather(key_tiles, "seq", axis=0, tiled=True),
        lax.all_gather(value_tiles, "seq", axis=0, tiled=True),
    )
    span_rows = pieces[0].shape[0]
    row_at = jnp.arange(span_rows, dtype=jnp.int32)
    select = (
        (row_at[None, :] // tile_dev == column_ids[:, None])
        & (row_at[None, :] % tile_dev == wanted[:, None])
    ).astype(jnp.bfloat16)
    new_keys = jnp.einsum("pn,ntw->ptw", select, pieces[0], preferred_element_type=jnp.float32)
    new_values = jnp.einsum("pn,ntw->ptw", select, pieces[1], preferred_element_type=jnp.float32)
    near_keys = new_keys.astype(jnp.bfloat16)
    near_values = new_values.astype(jnp.bfloat16)
    far_out = jnp.maximum(far_rank, 0)
    far_keys, far_values = (
        lax.all_to_all(
            jnp.take(key_tiles, far_out, axis=0), "grp", split_axis=0, concat_axis=0, tiled=True
        ),
        lax.all_to_all(
            jnp.take(value_tiles, far_out, axis=0), "grp", split_axis=0, concat_axis=0, tiled=True
        ),
    )
    own_slot = jnp.where(is_own, owner_rank, 0)
    near_slot = jnp.where(is_near, owner_column, 0)
    far_slot = jnp.where(is_far, owner_group, 0)
    own_pick = is_own[:, :, None, None]
    near_pick = is_near[:, :, None, None]
    far_pick = is_far[:, :, None, None]
    pair_width = 2 * HEAD_DIM
    score_scale = HEAD_DIM ** (-0.5)
    positions = jnp.arange(tile_rows)
    lower_mask = positions[None, :] <= positions[:, None]
    allowed = present[:, None, :, None] & (
        (my_flags == 0)[:, None, :, None] | lower_mask[None, :, None, :]
    )

    def spread(term, chosen_pick, slot, slots):
        total = jnp.zeros((slots, tile_rows, pair_width), jnp.float32)
        return total.at[slot].add(jnp.where(chosen_pick, term, 0.0)).astype(jnp.bfloat16)

    attended_parts = []
    query_parts = []
    own_key_parts = []
    near_key_parts = []
    far_key_parts = []
    own_value_parts = []
    near_value_parts = []
    far_value_parts = []
    for head_pair in range(HEADS // 2):
        start_col = head_pair * pair_width

        def columns_of(source):
            return source[..., start_col : start_col + pair_width]

        def fetch(own_source, near_source, far_source):
            from_own = jnp.take(columns_of(own_source), own_slot, axis=0)
            from_near = jnp.take(columns_of(near_source), near_slot, axis=0)
            from_far = jnp.take(columns_of(far_source), far_slot, axis=0)
            return jnp.where(own_pick, from_own, jnp.where(near_pick, from_near, from_far))

        key_block = fetch(key_tiles, near_keys, far_keys).reshape(
            tile_dev, entries, tile_rows, 2, HEAD_DIM
        )
        value_block = fetch(value_tiles, near_values, far_values).reshape(
            tile_dev, entries, tile_rows, 2, HEAD_DIM
        )
        query_block = columns_of(query_tiles).reshape(tile_dev, tile_rows, 2, HEAD_DIM)
        grad_block = columns_of(grad_tiles).reshape(tile_dev, tile_rows, 2, HEAD_DIM)
        scores = (
            jnp.einsum(
                "tihd,techd->thiec", query_block, key_block, preferred_element_type=jnp.float32
            )
            * score_scale
        )
        masked = jnp.where(allowed[:, None], scores, floor_score)
        row_top = jnp.max(masked, axis=(3, 4), keepdims=True)
        exponent = jnp.exp(masked - row_top)
        probs_exact = exponent / jnp.sum(exponent, axis=(3, 4), keepdims=True)
        probs = probs_exact.astype(jnp.bfloat16)
        attended_block = jnp.einsum(
            "thiec,techd->tihd", probs, value_block, preferred_element_type=jnp.float32
        ).astype(jnp.bfloat16)
        row_delta = jnp.sum(
            grad_block.astype(jnp.float32) * attended_block.astype(jnp.float32), axis=3
        )
        dprobs = jnp.einsum(
            "tihd,techd->thiec", grad_block, value_block, preferred_element_type=jnp.float32
        )
        dscores = (
            probs_exact * (dprobs - jnp.transpose(row_delta, (0, 2, 1))[..., None, None])
        ).astype(jnp.bfloat16)
        grad_query = (
            jnp.einsum("thiec,techd->tihd", dscores, key_block, preferred_element_type=jnp.float32)
            * score_scale
        )
        grad_key = (
            jnp.einsum(
                "thiec,tihd->techd", dscores, query_block, preferred_element_type=jnp.float32
            )
            * score_scale
        )
        grad_value = jnp.einsum(
            "thiec,tihd->techd", probs, grad_block, preferred_element_type=jnp.float32
        )
        grad_key = grad_key.reshape(tile_dev, entries, tile_rows, pair_width)
        grad_value = grad_value.reshape(tile_dev, entries, tile_rows, pair_width)
        attended_parts.append(attended_block.reshape(tile_dev, tile_rows, pair_width))
        query_parts.append(grad_query.astype(jnp.bfloat16).reshape(tile_dev, tile_rows, pair_width))
        own_key_parts.append(spread(grad_key, own_pick, own_slot, tile_dev))
        near_key_parts.append(spread(grad_key, near_pick, near_slot, columns))
        far_key_parts.append(spread(grad_key, far_pick, far_slot, groups))
        own_value_parts.append(spread(grad_value, own_pick, own_slot, tile_dev))
        near_value_parts.append(spread(grad_value, near_pick, near_slot, columns))
        far_value_parts.append(spread(grad_value, far_pick, far_slot, groups))

    def joined(parts):
        return jnp.concatenate(parts, axis=-1)

    near_back_keys, near_back_values = (
        lax.all_to_all(joined(near_key_parts), "seq", split_axis=0, concat_axis=0, tiled=True),
        lax.all_to_all(joined(near_value_parts), "seq", split_axis=0, concat_axis=0, tiled=True),
    )
    far_back_keys, far_back_values = (
        lax.all_to_all(joined(far_key_parts), "grp", split_axis=0, concat_axis=0, tiled=True),
        lax.all_to_all(joined(far_value_parts), "grp", split_axis=0, concat_axis=0, tiled=True),
    )
    near_onehot = (near_rank[None, :] == ranks[:, None]).astype(jnp.bfloat16)
    far_onehot = (far_rank[None, :] == ranks[:, None]).astype(jnp.bfloat16)

    def collect(own_part, near_back, far_back):
        total = own_part.astype(jnp.float32)
        total = total + jnp.einsum(
            "rp,ptw->rtw", near_onehot, near_back, preferred_element_type=jnp.float32
        )
        total = total + jnp.einsum(
            "rg,gtw->rtw", far_onehot, far_back, preferred_element_type=jnp.float32
        )
        return total.astype(jnp.bfloat16).reshape(1, tile_dev, 1, tile_rows, width)

    attended = joined(attended_parts).reshape(1, tile_dev, 1, tile_rows, width)
    grad_queries = joined(query_parts).reshape(1, tile_dev, 1, tile_rows, width)
    grad_keys = collect(joined(own_key_parts), near_back_keys, far_back_keys)
    grad_values = collect(joined(own_value_parts), near_back_values, far_back_values)
    return (attended, grad_queries, grad_keys, grad_values)


def solution(mesh):
    return jax.shard_map(
        per_device,
        mesh=mesh,
        in_specs=(
            P("grp", None, "seq", None, None),
            P("grp", None, "seq", None, None),
            P("grp", None, "seq", None, None),
            P("grp", None, "seq", None, None),
            P(),
            P(),
        ),
        out_specs=(
            P("grp", None, "seq", None, None),
            P("grp", None, "seq", None, None),
            P("grp", None, "seq", None, None),
            P("grp", None, "seq", None, None),
        ),
        check_vma=False,
    )
```

profile of v0, /device:TPU:1, one launch (start us, length us, event | category | flops | bytes accessed | tf_op | source)
XLA Modules:
  0.0 858.7 jit_solution(12798939972070502319)
XLA Ops:
  17.0 6.8 all-to-all-start
  29.0 10.0 %all-to-all-done = bf16[8,128,512]{2,1,0:T(8,128)(2,1)S(1)} async-done(((bf16[8,128,512]{2,1,0:T(8,128)(2,1)}), bf16[8,128,512]{2,1,0:T(8,128)(2,1)S(1)}, u32[]{:S(2)}, u32[]{:S(2)}) %all-to-all-start) | async-done | bytes 1048608 | tf_op jit(solution)/shard_map/all_to_all | solution.py:83
  39.0 5.0 all-to-all-start.1
  126.1 7.6 all-gather.5.cloned.1.call-done
  133.7 19.3 %fusion.26 = bf16[32,128,512]{2,0,1:T(8,128)(2,1)S(1)} fusion(bf16[1,96,1,128,512]{4,3,2,0,1:T(8,128)(2,1)} %all-gather.5.cloned.1.call-done, s32[96]{0:T(128)S(1)} %get-tuple-element.179, s32[96]{0:T(128)S(1)} %copy-done.72, s32[32]{0:T(128)S(1)} %select_reduce_fusion), kind=kOutput, calls=%fused_computation.121 | convolution fusion | flops 404759552 | bytes 16778112 | tf_op jit(solution)/shard_map/pn,ntw->ptw/dot_general | solution.py:75
  160.2 92.9 %all-gather.7.cloned.1.call-done = bf16[1,96,1,128,512]{4,3,2,0,1:T(8,128)(2,1)} async-done(((bf16[1,3,1,128,512]{4,3,2,0,1:T(8,128)(2,1)}), bf16[1,96,1,128,512]{4,3,2,0,1:T(8,128)(2,1)}) %all-gather.7.cloned.1.call-update) | async-done | bytes 12582928 | tf_op jit(solution)/shard_map/all_gather | solution.py:65
  253.1 19.1 %fusion.29 = bf16[32,128,512]{2,0,1:T(8,128)(2,1)S(1)} fusion(bf16[1,96,1,128,512]{4,3,2,0,1:T(8,128)(2,1)} %all-gather.7.cloned.1.call-done, s32[96]{0:T(128)S(1)} %get-tuple-element.179, s32[96]{0:T(128)S(1)} %copy-done.72, s32[32]{0:T(128)S(1)} %select_reduce_fusion), kind=kOutput, calls=%fused_computation.122 | convolution fusion | flops 404759552 | bytes 16778112 | tf_op jit(solution)/shard_map/pn,ntw->ptw/dot_general | solution.py:74
  316.8 8.7 %fusion.35 = (bf16[3,16,128,128]{2,3,1,0:T(8,128)(2,1)}, bf16[3,16,128,128]{2,3,1,0:T(8,128)(2,1)S(1)}, bf16[3,16,128,128]{2,3,1,0:T(8,128)(2,1)}, bf16[3,16,128,128]{2,3,1,0:T(8,128)(2,1)S(1)}) fusion(bf16[3,16,128,128]{2,3,1,0:T(8,128)(2,1)} %bitcast.460, bf16[3,16,128,128]{2,3,1,0:T(8,128)(2,1)} %copy.966, bf16[3,16,128,128]{2,3,1,0:T(8,128)(2,1)S(1)} %bitcast.452, ...), kind=kLoop, calls=%fused_computation.134 | loop fusion | flops 15728640 | bytes 25166064 | tf_op jit(solution)/shard_map/jit(_where)/select_n | solution.py:123
  331.0 4.9 fusion.39
  335.9 6.2 fusion.18
  342.2 6.1 fusion.11
  348.3 4.0 fusion.13
  355.2 3.5 convolution_bitcast_fusion
  358.8 3.2 fusion.6
  373.3 3.5 convolution_bitcast_fusion.2
  376.9 3.0 fusion.8
  379.9 3.0 multiply_reduce_fusion.3
  385.5 4.8 fusion.9
  409.9 32.1 %bitcast_select_fusion.18 = (f32[3,16,128,128]{2,3,1,0:T(8,128)}, f32[3,16,128,128]{2,3,1,0:T(8,128)}, f32[3,16,128,128]{2,3,1,0:T(8,128)}, f32[3,16,128,128]{2,...) fusion(f32[3,16,128,2,64]{2,4,3,1,0:T(8,128)S(1)} %copy.1022, ...), kind=kLoop, calls=%fused_computation.106 | loop fusion | flops 18874368 | bytes 100663440 | tf_op jit(solution)/shard_map/jit(_where)/select_n | solution.py:103
  442.1 3.5 copy.1033
  445.7 7.1 scatter_fusion.11
  452.8 3.6 copy.1032
  456.5 6.7 scatter_fusion.10
  463.9 3.6 copy.1031
  467.6 6.7 scatter_fusion.9
  475.1 3.6 copy.1030
  478.7 6.7 scatter_fusion.8
  487.7 5.3 all-to-all-start.3
  495.4 6.7 scatter_fusion.23
  502.2 3.5 copy.1056
  505.7 6.7 scatter_fusion.22
  513.2 3.7 copy.1055
  517.0 6.7 scatter_fusion.21
  524.4 3.6 copy.1054
  528.0 6.7 scatter_fusion.20
  537.1 5.0 all-to-all-start.5
  544.8 6.7 scatter_fusion.7
  551.7 3.6 copy.1026
  555.5 6.7 scatter_fusion.6
  563.4 3.6 copy.1025
  567.2 6.7 scatter_fusion.5
  575.0 3.6 copy.1024
  578.8 6.7 scatter_fusion.4
  589.3 5.8 all-to-all-start.2
  597.8 6.7 scatter_fusion.19
  604.7 3.6 copy.1050
  608.5 6.7 scatter_fusion.18
  616.4 3.5 copy.1049
  620.1 6.7 scatter_fusion.17
  628.0 3.5 copy.1048
  631.8 6.7 scatter_fusion.16
  642.3 45.9 %all-to-all-done.2 = bf16[32,128,512]{2,1,0:T(8,128)(2,1)} async-done(((bf16[32,128,512]{2,1,0:T(8,128)(2,1)}), bf16[32,128,512]{2,1,0:T(8,128)(2,1)}, u32[]{:S(2)}, u32[]{:S(2)}) %all-to-all-start.2) | async-done | bytes 4194336 | tf_op jit(solution)/shard_map/all_to_all | solution.py:184
  688.3 9.9 %all-to-all-start.4 = ((bf16[32,128,512]{2,1,0:T(8,128)(2,1)}), bf16[32,128,512]{2,1,0:T(8,128)(2,1)}, u32[]{:S(2)}, u32[]{:S(2)}) async-start(bf16[32,128,512]{2,1,0:T(8,128)(2,1)} %pad_maximum_fusion.1), calls=%async_computation.4 | async-start | bytes 8388608 | tf_op jit(solution)/shard_map/all_to_all | solution.py:185
  709.1 3.3 fusion.123
  719.1 10.2 %scatter_fusion.3 = f32[3,128,128]{2,1,0:T(8,128)} fusion(f32[3,128,128]{2,1,0:T(8,128)} %broadcast.258.clone, s32[48]{0:T(128)S(1)} %copy-done.41, f32[48,128,128]{2,1,0:T(8,128)S(1)} %copy.1023), kind=kCustom, calls=%fused_computation.31 | custom fusion | flops 786432 | bytes 9437376 | tf_op jit(solution)/shard_map/scatter-add | solution.py:103
  733.4 10.2 %scatter_fusion.2 = f32[3,128,128]{2,1,0:T(8,128)} fusion(f32[3,128,128]{2,1,0:T(8,128)} %broadcast.258.clone.1, s32[48]{0:T(128)S(1)} %copy-done.41, f32[48,128,128]{2,1,0:T(8,128)S(1)} %copy.1020), kind=kCustom, calls=%fused_computation.30 | custom fusion | flops 786432 | bytes 9437376 | tf_op jit(solution)/shard_map/scatter-add | solution.py:103
  747.6 10.2 %scatter_fusion.1 = f32[3,128,128]{2,1,0:T(8,128)} fusion(f32[3,128,128]{2,1,0:T(8,128)} %broadcast.258.clone.2, s32[48]{0:T(128)S(1)} %copy-done.41, f32[48,128,128]{2,1,0:T(8,128)S(1)} %copy.1017), kind=kCustom, calls=%fused_computation.29 | custom fusion | flops 786432 | bytes 9437376 | tf_op jit(solution)/shard_map/scatter-add | solution.py:103
  761.8 10.2 %scatter_fusion = f32[3,128,128]{2,1,0:T(8,128)} fusion(f32[3,128,128]{2,1,0:T(8,128)} %broadcast.258.clone.3, s32[48]{0:T(128)S(1)} %copy-done.41, f32[48,128,128]{2,1,0:T(8,128)S(1)} %copy.1014), kind=kCustom, calls=%fused_computation.28 | custom fusion | flops 786432 | bytes 9437376 | tf_op jit(solution)/shard_map/scatter-add | solution.py:103
  776.7 10.2 %scatter_fusion.15 = f32[3,128,128]{2,1,0:T(8,128)} fusion(f32[3,128,128]{2,1,0:T(8,128)} %broadcast.258.clone.4, s32[48]{0:T(128)S(1)} %copy-done.41, f32[48,128,128]{2,1,0:T(8,128)S(1)} %copy.1047), kind=kCustom, calls=%fused_computation.43 | custom fusion | flops 786432 | bytes 9437376 | tf_op jit(solution)/shard_map/scatter-add | solution.py:103
  791.0 10.2 %scatter_fusion.14 = f32[3,128,128]{2,1,0:T(8,128)} fusion(f32[3,128,128]{2,1,0:T(8,128)} %broadcast.258.clone.5, s32[48]{0:T(128)S(1)} %copy-done.41, f32[48,128,128]{2,1,0:T(8,128)S(1)} %copy.1044), kind=kCustom, calls=%fused_computation.42 | custom fusion | flops 786432 | bytes 9437376 | tf_op jit(solution)/shard_map/scatter-add | solution.py:103
  805.8 10.2 %scatter_fusion.13 = f32[3,128,128]{2,1,0:T(8,128)} fusion(f32[3,128,128]{2,1,0:T(8,128)} %broadcast.258.clone.6, s32[48]{0:T(128)S(1)} %copy-done.41, f32[48,128,128]{2,1,0:T(8,128)S(1)} %copy.1041), kind=kCustom, calls=%fused_computation.41 | custom fusion | flops 786432 | bytes 9437376 | tf_op jit(solution)/shard_map/scatter-add | solution.py:103
  820.9 10.2 %scatter_fusion.12 = f32[3,128,128]{2,1,0:T(8,128)} fusion(f32[3,128,128]{2,1,0:T(8,128)} %broadcast.258.clone.7, s32[48]{0:T(128)S(1)} %copy-done.41, f32[48,128,128]{2,1,0:T(8,128)S(1)} %copy.1038), kind=kCustom, calls=%fused_computation.40 | custom fusion | flops 786432 | bytes 9437376 | tf_op jit(solution)/shard_map/scatter-add | solution.py:103
  839.7 4.6 fusion.24
  845.6 4.6 fusion.22
  (367 shorter events, 278.3 us)
Async XLA Ops:
  7.2 5.2 copy-start.12
  7.2 126.5 %all-gather.5.cloned.1.call-start = ((), (), s32[]{:S(2)}) async-start(), calls=%async_computation.6 | async-start | bytes 12976128 | tf_op jit(solution)/shard_map/all_gather | solution.py:66
  7.9 245.2 %all-gather.7.cloned.1.call-start = ((), (), s32[]{:S(2)}) async-start(), calls=%async_computation.7 | async-start | bytes 12976128 | tf_op jit(solution)/shard_map/all_gather | solution.py:65
  14.0 9.8 %copy-start.56 = (s32[768,16]{0,1:T(8,128)S(1)}, s32[768,16]{0,1:T(8,128)}, u32[]{:S(2)}) copy-start(s32[768,16]{0,1:T(8,128)} %param.20) | copy-start | bytes 147460
  14.0 10.0 %copy-start.65 = (s32[768,16]{0,1:T(8,128)S(1)}, s32[768,16]{0,1:T(8,128)}, u32[]{:S(2)}) copy-start(s32[768,16]{0,1:T(8,128)} %param.21) | copy-start | bytes 147460
  14.0 13.3 %copy-start.13 = (bf16[1,3,1,128,512]{4,3,2,1,0:T(8,128)(2,1)S(1)}, bf16[1,3,1,128,512]{4,3,2,1,0:T(8,128)(2,1)}, u32[]{:S(2)}) copy-start(bf16[1,3,1,128,512]{4,3,2,1,0:T(8,128)(2,1)} %param.17) | copy-start | bytes 1179652
  17.0 10.4 %copy-start.51 = (bf16[1,3,1,128,512]{4,3,2,1,0:T(8,128)(2,1)S(1)}, bf16[1,3,1,128,512]{4,3,2,1,0:T(8,128)(2,1)}, u32[]{:S(2)}) copy-start(bf16[1,3,1,128,512]{4,3,2,1,0:T(8,128)(2,1)} %param.19) | copy-start | bytes 1179652
  17.0 11.2 %copy-start.52 = (bf16[1,3,1,128,512]{4,3,2,1,0:T(8,128)(2,1)S(1)}, bf16[1,3,1,128,512]{4,3,2,1,0:T(8,128)(2,1)}, u32[]{:S(2)}) copy-start(bf16[1,3,1,128,512]{4,3,2,1,0:T(8,128)(2,1)} %param.16) | copy-start | bytes 1179652
  17.0 21.9 %all-to-all-start = ((bf16[8,128,512]{2,1,0:T(8,128)(2,1)}), bf16[8,128,512]{2,1,0:T(8,128)(2,1)S(1)}, u32[]{:S(2)}, u32[]{:S(2)}) async-start(bf16[8,128,512]{2,1,0:T(8,128)(2,1)} %get-tuple-element.167), calls=%async_computation | async-start | bytes 2097152 | tf_op jit(solution)/shard_map/all_to_all | solution.py:83
  26.0 302.3 %copy-start.68 = (pred[3,16]{1,0:T(4,128)(4,1)}, pred[3,16]{1,0:T(4,128)(4,1)S(1)}, u32[]{:S(2)}) copy-start(pred[3,16]{1,0:T(4,128)(4,1)S(1)} %get-tuple-element.61) | copy-start | bytes 148
  26.5 301.8 %copy-start.66 = (pred[3,16]{1,0:T(4,128)(4,1)}, pred[3,16]{1,0:T(4,128)(4,1)S(1)}, u32[]{:S(2)}) copy-start(pred[3,16]{1,0:T(4,128)(4,1)S(1)} %get-tuple-element.69) | copy-start | bytes 148
  39.0 11.1 %copy-start.24 = (bf16[8,128,512]{2,1,0:T(8,128)(2,1)}, bf16[8,128,512]{2,1,0:T(8,128)(2,1)S(1)}, u32[]{:S(2)}) copy-start(bf16[8,128,512]{2,1,0:T(8,128)(2,1)S(1)} %all-to-all-done) | copy-start | bytes 3145732
  39.0 53.7 %all-to-all-start.1 = ((bf16[8,128,512]{2,1,0:T(8,128)(2,1)}), bf16[8,128,512]{2,1,0:T(8,128)(2,1)}, u32[]{:S(2)}, u32[]{:S(2)}) async-start(bf16[8,128,512]{2,1,0:T(8,128)(2,1)} %get-tuple-element.166), calls=%async_computation.1 | async-start | bytes 2097152 | tf_op jit(solution)/shard_map/all_to_all | solution.py:80
  46.1 38.6 %copy-start.42 = (s32[48]{0:T(128)}, s32[48]{0:T(128)S(1)}, u32[]{:S(2)}) copy-start(s32[48]{0:T(128)S(1)} %reshape.872) | copy-start | bytes 580
  59.3 4.6 copy-start.55
  64.1 261.5 %copy-start.36 = (bf16[3,128,128]{1,2,0:T(8,128)(2,1)}, bf16[3,128,128]{1,2,0:T(8,128)(2,1)S(1)}, u32[]{:S(2)}) copy-start(bf16[3,128,128]{1,2,0:T(8,128)(2,1)S(1)} %copy.972) | copy-start | bytes 294916
  75.9 8.1 copy-start.53
  75.9 9.0 %copy-start.73 = (pred[3,16]{1,0:T(4,128)(4,1)S(1)}, pred[3,16]{1,0:T(4,128)(4,1)}, u32[]{:S(2)}) copy-start(pred[3,16]{1,0:T(4,128)(4,1)} %get-tuple-element.165) | copy-start | bytes 148
  76.7 6.5 copy-start.54
  121.4 12.3 %copy-start.72 = (s32[96]{0:T(128)S(1)}, s32[96]{0:T(128)}, u32[]{:S(2)}) copy-start(s32[96]{0:T(128)} %get-tuple-element.180) | copy-start | bytes 1156
  327.2 2.9 copy-start.20
  327.2 3.4 copy-start.21
  327.2 3.8 copy-start.22
  331.0 4.9 copy-start.46
  335.9 6.3 copy-start.14
  335.9 6.3 copy-start.15
  335.9 6.3 copy-start.29
  335.9 6.3 copy-start.47
  348.2 4.0 copy-start.35
  348.2 4.0 copy-start.61
  358.8 3.3 copy-start.33
  358.8 3.3 copy-start.64
  362.0 28.3 %copy-start.4 = (bf16[3,2,128,16,128]{2,4,3,1,0:T(8,128)(2,1)}, bf16[3,2,128,16,128]{2,4,3,1,0:T(8,128)(2,1)S(1)}, u32[]{:S(2)}) copy-start(bf16[3,2,128,16,128]{2,4,3,1,0:T(8,128)(2,1)S(1)} %fusion.6) | copy-start | bytes 9437188
  367.5 2.9 copy-start.34
  367.5 2.9 copy-start.63
  370.4 36.5 %copy-start.5 = (bf16[3,2,128,16,128]{2,4,3,1,0:T(8,128)(2,1)}, bf16[3,2,128,16,128]{2,4,3,1,0:T(8,128)(2,1)S(1)}, u32[]{:S(2)}) copy-start(bf16[3,2,128,16,128]{2,4,3,1,0:T(8,128)(2,1)S(1)} %fusion.7) | copy-start | bytes 9437188
  373.3 6.5 slice-start
  376.9 3.0 copy-start.32
  376.9 3.0 copy-start.62
  376.9 3.0 slice-start.1
  379.9 23.9 %copy-start.6 = (bf16[3,2,128,16,128]{2,4,3,1,0:T(8,128)(2,1)}, bf16[3,2,128,16,128]{2,4,3,1,0:T(8,128)(2,1)S(1)}, u32[]{:S(2)}) copy-start(bf16[3,2,128,16,128]{2,4,3,1,0:T(8,128)(2,1)S(1)} %fusion.8) | copy-start | bytes 9437188
  385.5 4.8 copy-start.39
  390.3 10.4 %copy-start.7 = (bf16[3,2,128,16,128]{2,4,3,1,0:T(8,128)(2,1)}, bf16[3,2,128,16,128]{2,4,3,1,0:T(8,128)(2,1)S(1)}, u32[]{:S(2)}) copy-start(bf16[3,2,128,16,128]{2,4,3,1,0:T(8,128)(2,1)S(1)} %fusion.9) | copy-start | bytes 9437188
  395.7 3.0 copy-start.30
  442.1 3.6 copy-start.45
  485.4 7.6 copy-start.11
  487.7 49.4 %all-to-all-start.3 = ((bf16[8,128,512]{2,1,0:T(8,128)(2,1)}), bf16[8,128,512]{2,1,0:T(8,128)(2,1)}, u32[]{:S(2)}, u32[]{:S(2)}) async-start(bf16[8,128,512]{2,1,0:T(8,128)(2,1)} %pad_maximum_fusion.2), calls=%async_computation.3 | async-start | bytes 2097152 | tf_op jit(solution)/shard_map/all_to_all | solution.py:188
  534.8 7.4 copy-start.10
  537.1 52.2 %all-to-all-start.5 = ((bf16[8,128,512]{2,1,0:T(8,128)(2,1)}), bf16[8,128,512]{2,1,0:T(8,128)(2,1)}, u32[]{:S(2)}, u32[]{:S(2)}) async-start(bf16[8,128,512]{2,1,0:T(8,128)(2,1)} %pad_maximum_fusion.3), calls=%async_computation.5 | async-start | bytes 2097152 | tf_op jit(solution)/shard_map/all_to_all | solution.py:189
  589.3 5.8 copy-start.9
  589.3 98.9 %all-to-all-start.2 = ((bf16[32,128,512]{2,1,0:T(8,128)(2,1)}), bf16[32,128,512]{2,1,0:T(8,128)(2,1)}, u32[]{:S(2)}, u32[]{:S(2)}) async-start(bf16[32,128,512]{2,1,0:T(8,128)(2,1)} %pad_maximum_fusion), calls=%async_computation.2 | async-start | bytes 8388608 | tf_op jit(solution)/shard_map/all_to_all | solution.py:184
  642.3 57.0 %copy-start.57 = (bf16[3,2,64,128]{3,2,1,0:T(8,128)(2,1)S(1)}, bf16[3,2,64,128]{3,2,1,0:T(8,128)(2,1)}, u32[]{:S(2)}) copy-start(bf16[3,2,64,128]{3,2,1,0:T(8,128)(2,1)} %get-tuple-element.172) | copy-start | bytes 294916
  642.3 57.7 %copy-start.58 = (bf16[3,2,64,128]{3,2,1,0:T(8,128)(2,1)S(1)}, bf16[3,2,64,128]{3,2,1,0:T(8,128)(2,1)}, u32[]{:S(2)}) copy-start(bf16[3,2,64,128]{3,2,1,0:T(8,128)(2,1)} %get-tuple-element.174) | copy-start | bytes 294916
  642.3 58.5 %copy-start.59 = (bf16[3,2,64,128]{3,2,1,0:T(8,128)(2,1)S(1)}, bf16[3,2,64,128]{3,2,1,0:T(8,128)(2,1)}, u32[]{:S(2)}) copy-start(bf16[3,2,64,128]{3,2,1,0:T(8,128)(2,1)} %get-tuple-element.176) | copy-start | bytes 294916
  642.3 59.3 %copy-start.60 = (bf16[3,2,64,128]{3,2,1,0:T(8,128)(2,1)S(1)}, bf16[3,2,64,128]{3,2,1,0:T(8,128)(2,1)}, u32[]{:S(2)}) copy-start(bf16[3,2,64,128]{3,2,1,0:T(8,128)(2,1)} %get-tuple-element.178) | copy-start | bytes 294916
  642.3 60.0 %copy-start.3 = (bf16[3,16,128,128]{2,3,1,0:T(8,128)(2,1)S(1)}, bf16[3,16,128,128]{2,3,1,0:T(8,128)(2,1)}, u32[]{:S(2)}) copy-start(bf16[3,16,128,128]{2,3,1,0:T(8,128)(2,1)} %copy-done.2) | copy-start | bytes 4718596
  688.3 157.3 %all-to-all-start.4 = ((bf16[32,128,512]{2,1,0:T(8,128)(2,1)}), bf16[32,128,512]{2,1,0:T(8,128)(2,1)}, u32[]{:S(2)}, u32[]{:S(2)}) async-start(bf16[32,128,512]{2,1,0:T(8,128)(2,1)} %pad_maximum_fusion.1), calls=%async_computation.4 | async-start | bytes 8388608 | tf_op jit(solution)/shard_map/all_to_all | solution.py:185
  698.2 7.5 copy-start.1
  708.3 4.8 copy-start.8
  716.0 3.1 copy-start.41
  820.9 14.8 %copy-start.71 = (s32[8]{0:T(128)S(1)}, s32[8]{0:T(128)}, u32[]{:S(2)}) copy-start(s32[8]{0:T(128)} %copy-done.70) | copy-start | bytes 100
  839.7 4.6 copy-start.48
  845.6 4.7 copy-start.49
  845.6 4.7 copy-start.50
  (21 other events, 35.3 us)
Sparse Core Ops, SparseCore 0:
  10.6 123.0 all-gather.4
  136.3 116.7 all-gather.6
where the time goes:
time: 874 us; the launch traced here: 859 us
  other arithmetic  280 us (32%)
  local copies, waits for them, and re-layouts  247 us (28%)
  waiting for transfers between devices  158 us (18%)
  matrix products  120 us (14%)
  starting transfers between devices  37.9 us (4%)
  between operations  15.9 us (2%)
    scatter-add x24, other arithmetic, spread(): total.at[slot].add(jnp.where(chosen_pick, term, 0.0)).astype(jnp.bfloat16)  190 us
    all_gather x1, waiting for transfers between devices, per_device(): lax.all_gather(key_tiles, 'seq', axis=0, tiled=True)  92.9 us
    select_n x24, local copies, waits for them, and re-layouts, spread(): jnp.where(chosen_pick, term, 0.0)  72.8 us
    all_to_all x1, waiting for transfers between devices, per_device(): lax.all_to_all(joined(near_key_parts), 'seq', split_axis=0, concat_axis=0...  45.9 us
    gather x16, local copies, waits for them, and re-layouts, fetch(): from_near = jnp.take(columns_of(near_source), near_slot, axis=0)  36.9 us
    gather x16, local copies, waits for them, and re-layouts, fetch(): from_far = jnp.take(columns_of(far_source), far_slot, axis=0)  36.7 us
    select_n x1, other arithmetic, spread(): jnp.where(chosen_pick, term, 0.0)  32.1 us
    gather x16, local copies, waits for them, and re-layouts, fetch(): from_own = jnp.take(columns_of(own_source), own_slot, axis=0)  32 us
  transfers between devices with their start and end apart: 8, of which 4 were waited for; matrix products, arithmetic and copies ran while one was open for 47% of the time, Pallas kernels for 0%

commit v1 on v0

--- a/solution.py
+++ b/solution.py
@@ -6,6 +6,14 @@
 HEADS = 8
 HEAD_DIM = 64
 floor_score = -1e30
+
+
+def gather_from_all(shard, axis, dim):
+    size = lax.axis_size(axis)
+    repeats = [size if d == dim else 1 for d in range(shard.ndim)]
+    return lax.all_to_all(
+        jnp.tile(shard, repeats), axis, split_axis=dim, concat_axis=dim, tiled=True
+    )
 
 
 def locate(entry_ids, group_tiles, columns):
@@ -62,7 +70,7 @@
         axis=(0, 1),
     )
     pieces = (
-        lax.all_gather(key_tiles, "seq", axis=0, tiled=True),
+        gather_from_all(key_tiles, "seq", 0),
         lax.all_gather(value_tiles, "seq", axis=0, tiled=True),
     )
     span_rows = pieces[0].shape[0]

time: 874 us -> 1030 us (1.18)
  waiting for transfers between devices: 158 us -> 289 us
  blocking collectives: 0 us -> 19 us
  starting transfers between devices: 37.9 us -> 48.2 us
    all_gather x1, waiting for transfers between devices: 7.58 us -> 133 us  [per_device(): lax.all_gather(value_tiles, 'seq', axis=0, tiled=True)]
    all_to_all x1, waiting for transfers between devices: 0.01 us -> 94.1 us  [gather_from_all(): lax.all_to_all(jnp.tile(shard, repeats), axis, split_axis=dim, concat_axi...]
    all_gather x1 -> x0, waiting for transfers between devices: 92.9 us -> none  [per_device(): lax.all_gather(key_tiles, 'seq', axis=0, tiled=True)]
    all_to_all x0 -> x1, blocking collectives: none -> 19 us  [per_device(): lax.all_to_all(jnp.take(key_tiles, far_out, axis=0), 'grp', split_axis=0,...]
  transfers between devices with their start and end apart: 8 -> 7, of which waited for: 4 -> 4; matrix products, arithmetic and copies ran while one was open for 47% -> 39% of each run, Pallas kernels for 0% -> 0%
where the time goes in v1:
time: 1030 us; the launch traced here: 1020 us
  waiting for transfers between devices  289 us (28%)
  other arithmetic  277 us (27%)
  local copies, waits for them, and re-layouts  251 us (24%)
  matrix products  119 us (12%)
  starting transfers between devices  48.2 us (5%)
  blocking collectives  19 us (2%)
  between operations  15.9 us (2%)
    scatter-add x24, other arithmetic, spread(): total.at[slot].add(jnp.where(chosen_pick, term, 0.0)).astype(jnp.bfloat16)  190 us
    all_gather x1, waiting for transfers between devices, per_device(): lax.all_gather(value_tiles, 'seq', axis=0, tiled=True)  133 us
    all_to_all x1, waiting for transfers between devices, gather_from_all(): lax.all_to_all(jnp.tile(shard, repeats), axis, split_axis=dim, concat_axi...  94.1 us
    select_n x24, local copies, waits for them, and re-layouts, spread(): jnp.where(chosen_pick, term, 0.0)  72.8 us
    all_to_all x1, waiting for transfers between devices, per_device(): lax.all_to_all(joined(near_key_parts), 'seq', split_axis=0, concat_axis=0...  45.9 us
    gather x16, local copies, waits for them, and re-layouts, fetch(): from_far = jnp.take(columns_of(far_source), far_slot, axis=0)  36.5 us
    gather x16, local copies, waits for them, and re-layouts, fetch(): from_near = jnp.take(columns_of(near_source), near_slot, axis=0)  36.5 us
    select_n x1, other arithmetic, spread(): jnp.where(chosen_pick, term, 0.0)  32.1 us
  transfers between devices with their start and end apart: 7, of which 4 were waited for; matrix products, arithmetic and copies ran while one was open for 39% of the time, Pallas kernels for 0%

profile of v1, /device:TPU:1, one launch (start us, length us, event | category | flops | bytes accessed | tf_op | source)
XLA Modules:
  0.0 1019.9 jit_solution(17583719161888511018)
XLA Ops:
  12.9 6.8 all-to-all-start
  20.5 14.4 %all-to-all-done = bf16[8,128,512]{2,1,0:T(8,128)(2,1)S(1)} async-done(((bf16[8,128,512]{2,1,0:T(8,128)(2,1)}), bf16[8,128,512]{2,1,0:T(8,128)(2,1)S(1)}, u32[]{:S(2)}, u32[]{:S(2)}) %all-to-all-start) | async-done | bytes 1048608 | tf_op jit(solution)/shard_map/all_to_all | solution.py:91
  34.9 19.0 %all_to_all.35 = bf16[8,128,512]{2,1,0:T(8,128)(2,1)} all-to-all(bf16[8,128,512]{2,1,0:T(8,128)(2,1)S(1)} %get-tuple-element.166), channel_id=1, replica_groups=mesh['grp'=8,'seq'=32] {'grp'}, dimensions={0} | all-to-all | bytes 2097152 | tf_op jit(solution)/shard_map/all_to_all | solution.py:88
  53.9 6.1 tile.8
  60.0 11.1 %all-to-all-start.1 = ((bf16[96,128,512]{2,1,0:T(8,128)(2,1)}), bf16[96,128,512]{2,1,0:T(8,128)(2,1)}, u32[]{:S(2)}, u32[]{:S(2)}) async-start(bf16[96,128,512]{2,1,0:T(8,128)(2,1)} %bitcast.405), calls=%async_computation.1 | async-start | bytes 25165824 | tf_op jit(solution)/shard_map/all_to_all | solution.py:14
  156.4 133.4 %all-gather.3.cloned.1.call-done = bf16[1,96,1,128,512]{4,3,2,0,1:T(8,128)(2,1)} async-done(((bf16[1,3,1,128,512]{4,3,2,0,1:T(8,128)(2,1)}), bf16[1,96,1,128,512]{4,3,2,0,1:T(8,128)(2,1)}) %all-gather.3.cloned.1.call-update) | async-done | bytes 12582928 | tf_op jit(solution)/shard_map/all_gather | solution.py:74
  289.9 19.3 %fusion.28 = bf16[32,128,512]{2,0,1:T(8,128)(2,1)S(1)} fusion(bf16[1,96,1,128,512]{4,3,2,0,1:T(8,128)(2,1)} %all-gather.3.cloned.1.call-done, s32[96]{0:T(128)S(1)} %get-tuple-element.179, s32[96]{0:T(128)S(1)} %get-tuple-element.180, s32[32]{0:T(128)S(1)} %select_reduce_fusion), kind=kOutput, calls=%fused_computation.121 | convolution fusion | flops 404759552 | bytes 16778112 | tf_op jit(solution)/shard_map/pn,ntw->ptw/dot_general | solution.py:83
  316.3 94.1 %all-to-all-done.1 = bf16[96,128,512]{2,1,0:T(8,128)(2,1)} async-done(((bf16[96,128,512]{2,1,0:T(8,128)(2,1)}), bf16[96,128,512]{2,1,0:T(8,128)(2,1)}, u32[]{:S(2)}, u32[]{:S(2)}) %all-to-all-start.1) | async-done | bytes 12582944 | tf_op jit(solution)/shard_map/all_to_all | solution.py:14
  410.4 19.1 %fusion.25 = bf16[32,128,512]{2,0,1:T(8,128)(2,1)S(1)} fusion(bf16[96,128,512]{2,1,0:T(8,128)(2,1)} %all-to-all-done.1, s32[96]{0:T(128)S(1)} %get-tuple-element.179, s32[96]{0:T(128)S(1)} %get-tuple-element.180, s32[32]{0:T(128)S(1)} %select_reduce_fusion), kind=kOutput, calls=%fused_computation.120 | convolution fusion | flops 404759552 | bytes 16778112 | tf_op jit(solution)/shard_map/pn,ntw->ptw/dot_general | solution.py:82
  473.8 8.8 fusion.34
  488.1 4.9 fusion.38
  493.0 6.2 fusion.17
  499.2 6.1 fusion.10
  505.3 4.0 fusion.12
  512.2 3.5 convolution_bitcast_fusion
  515.8 3.2 fusion.5
  530.3 3.5 convolution_bitcast_fusion.2
  542.4 4.8 fusion.8
  566.9 32.1 %bitcast_select_fusion.18 = (f32[3,16,128,128]{2,3,1,0:T(8,128)}, f32[3,16,128,128]{2,3,1,0:T(8,128)}, f32[3,16,128,128]{2,3,1,0:T(8,128)}, f32[3,16,128,128]{2,...) fusion(f32[3,16,128,2,64]{2,4,3,1,0:T(8,128)S(1)} %copy.1019, ...), kind=kLoop, calls=%fused_computation.105 | loop fusion | flops 18874368 | bytes 100663440 | tf_op jit(solution)/shard_map/jit(_where)/select_n | solution.py:111
  599.1 3.5 copy.1030
  602.6 7.1 scatter_fusion.11
  609.8 3.6 copy.1029
  613.5 6.7 scatter_fusion.10
  620.9 3.6 copy.1028
  624.6 6.7 scatter_fusion.9
  632.1 3.6 copy.1027
  635.7 6.7 scatter_fusion.8
  644.7 5.6 all-to-all-start.4
  652.7 6.7 scatter_fusion.23
  659.5 3.5 copy.1053
  663.0 6.7 scatter_fusion.22
  670.5 3.7 copy.1052
  674.3 6.7 scatter_fusion.21
  681.7 3.6 copy.1051
  685.3 6.7 scatter_fusion.20
  694.4 5.1 all-to-all-start.6
  702.1 6.7 scatter_fusion.7
  709.0 3.5 copy.1023
  712.8 6.7 scatter_fusion.6
  720.6 3.5 copy.1022
  724.4 6.7 scatter_fusion.5
  732.3 3.5 copy.1021
  736.1 6.7 scatter_fusion.4
  746.6 9.7 all-to-all-start.3
  759.0 6.7 scatter_fusion.19
  765.8 3.6 copy.1047
  769.7 6.7 scatter_fusion.18
  777.5 3.5 copy.1046
  781.3 6.7 scatter_fusion.17
  789.2 3.5 copy.1045
  793.0 6.7 scatter_fusion.16
  803.5 45.9 %all-to-all-done.3 = bf16[32,128,512]{2,1,0:T(8,128)(2,1)} async-done(((bf16[32,128,512]{2,1,0:T(8,128)(2,1)}), bf16[32,128,512]{2,1,0:T(8,128)(2,1)}, u32[]{:S(2)}, u32[]{:S(2)}) %all-to-all-start.3) | async-done | bytes 4194336 | tf_op jit(solution)/shard_map/all_to_all | solution.py:192
  849.5 9.9 all-to-all-start.5
  870.3 3.3 fusion.122
  880.3 10.2 %scatter_fusion.3 = f32[3,128,128]{2,1,0:T(8,128)} fusion(f32[3,128,128]{2,1,0:T(8,128)} %broadcast.260.clone, s32[48]{0:T(128)S(1)} %copy-done.42, f32[48,128,128]{2,1,0:T(8,128)S(1)} %copy.1020), kind=kCustom, calls=%fused_computation.31 | custom fusion | flops 786432 | bytes 9437376 | tf_op jit(solution)/shard_map/scatter-add | solution.py:111
  894.6 10.2 %scatter_fusion.2 = f32[3,128,128]{2,1,0:T(8,128)} fusion(f32[3,128,128]{2,1,0:T(8,128)} %broadcast.260.clone.1, s32[48]{0:T(128)S(1)} %copy-done.42, f32[48,128,128]{2,1,0:T(8,128)S(1)} %copy.1017), kind=kCustom, calls=%fused_computation.30 | custom fusion | flops 786432 | bytes 9437376 | tf_op jit(solution)/shard_map/scatter-add | solution.py:111
  908.8 10.2 %scatter_fusion.1 = f32[3,128,128]{2,1,0:T(8,128)} fusion(f32[3,128,128]{2,1,0:T(8,128)} %broadcast.260.clone.2, s32[48]{0:T(128)S(1)} %copy-done.42, f32[48,128,128]{2,1,0:T(8,128)S(1)} %copy.1014), kind=kCustom, calls=%fused_computation.29 | custom fusion | flops 786432 | bytes 9437376 | tf_op jit(solution)/shard_map/scatter-add | solution.py:111
  923.1 10.2 %scatter_fusion = f32[3,128,128]{2,1,0:T(8,128)} fusion(f32[3,128,128]{2,1,0:T(8,128)} %broadcast.260.clone.3, s32[48]{0:T(128)S(1)} %copy-done.42, f32[48,128,128]{2,1,0:T(8,128)S(1)} %copy.1011), kind=kCustom, calls=%fused_computation.28 | custom fusion | flops 786432 | bytes 9437376 | tf_op jit(solution)/shard_map/scatter-add | solution.py:111
  937.9 10.2 %scatter_fusion.15 = f32[3,128,128]{2,1,0:T(8,128)} fusion(f32[3,128,128]{2,1,0:T(8,128)} %broadcast.260.clone.4, s32[48]{0:T(128)S(1)} %copy-done.42, f32[48,128,128]{2,1,0:T(8,128)S(1)} %copy.1044), kind=kCustom, calls=%fused_computation.43 | custom fusion | flops 786432 | bytes 9437376 | tf_op jit(solution)/shard_map/scatter-add | solution.py:111
  952.2 10.2 %scatter_fusion.14 = f32[3,128,128]{2,1,0:T(8,128)} fusion(f32[3,128,128]{2,1,0:T(8,128)} %broadcast.260.clone.5, s32[48]{0:T(128)S(1)} %copy-done.42, f32[48,128,128]{2,1,0:T(8,128)S(1)} %copy.1041), kind=kCustom, calls=%fused_computation.42 | custom fusion | flops 786432 | bytes 9437376 | tf_op jit(solution)/shard_map/scatter-add | solution.py:111
  967.0 10.2 %scatter_fusion.13 = f32[3,128,128]{2,1,0:T(8,128)} fusion(f32[3,128,128]{2,1,0:T(8,128)} %broadcast.260.clone.6, s32[48]{0:T(128)S(1)} %copy-done.42, f32[48,128,128]{2,1,0:T(8,128)S(1)} %copy.1038), kind=kCustom, calls=%fused_computation.41 | custom fusion | flops 786432 | bytes 9437376 | tf_op jit(solution)/shard_map/scatter-add | solution.py:111
  982.2 10.2 %scatter_fusion.12 = f32[3,128,128]{2,1,0:T(8,128)} fusion(f32[3,128,128]{2,1,0:T(8,128)} %broadcast.260.clone.7, s32[48]{0:T(128)S(1)} %copy-done.42, f32[48,128,128]{2,1,0:T(8,128)S(1)} %copy.1035), kind=kCustom, calls=%fused_computation.40 | custom fusion | flops 786432 | bytes 9437376 | tf_op jit(solution)/shard_map/scatter-add | solution.py:111
  1000.9 4.6 fusion.23
  1006.8 4.6 fusion.21
  (362 shorter events, 278.6 us)
Async XLA Ops:
  7.2 3.9 copy-start.13
  12.9 41.0 %copy-start.12 = (bf16[1,3,1,128,512]{4,3,2,1,0:T(8,128)(2,1)S(1)}, bf16[1,3,1,128,512]{4,3,2,1,0:T(8,128)(2,1)}, u32[]{:S(2)}) copy-start(bf16[1,3,1,128,512]{4,3,2,1,0:T(8,128)(2,1)} %param.17) | copy-start | bytes 1179652
  12.9 21.9 %all-to-all-start = ((bf16[8,128,512]{2,1,0:T(8,128)(2,1)}), bf16[8,128,512]{2,1,0:T(8,128)(2,1)S(1)}, u32[]{:S(2)}, u32[]{:S(2)}) async-start(bf16[8,128,512]{2,1,0:T(8,128)(2,1)} %get-tuple-element.167), calls=%async_computation | async-start | bytes 2097152 | tf_op jit(solution)/shard_map/all_to_all | solution.py:91
  19.7 270.1 %all-gather.3.cloned.1.call-start = ((), (), s32[]{:S(2)}) async-start(), calls=%async_computation.7 | async-start | bytes 12976128 | tf_op jit(solution)/shard_map/all_gather | solution.py:74
  34.9 25.1 %copy-start.25 = (bf16[8,128,512]{2,1,0:T(8,128)(2,1)}, bf16[8,128,512]{2,1,0:T(8,128)(2,1)S(1)}, u32[]{:S(2)}) copy-start(bf16[8,128,512]{2,1,0:T(8,128)(2,1)S(1)} %all-to-all-done) | copy-start | bytes 3145732
  60.0 11.1 %copy-start.56 = (s32[768,16]{0,1:T(8,128)S(1)}, s32[768,16]{0,1:T(8,128)}, u32[]{:S(2)}) copy-start(s32[768,16]{0,1:T(8,128)} %param.20) | copy-start | bytes 147460
  60.0 11.3 %copy-start.52 = (bf16[1,3,1,128,512]{4,3,2,1,0:T(8,128)(2,1)S(1)}, bf16[1,3,1,128,512]{4,3,2,1,0:T(8,128)(2,1)}, u32[]{:S(2)}) copy-start(bf16[1,3,1,128,512]{4,3,2,1,0:T(8,128)(2,1)} %param.19) | copy-start | bytes 1179652
  60.0 12.8 %copy-start.65 = (s32[768,16]{0,1:T(8,128)S(1)}, s32[768,16]{0,1:T(8,128)}, u32[]{:S(2)}) copy-start(s32[768,16]{0,1:T(8,128)} %param.21) | copy-start | bytes 147460
  60.0 14.1 %copy-start.53 = (bf16[1,3,1,128,512]{4,3,2,1,0:T(8,128)(2,1)S(1)}, bf16[1,3,1,128,512]{4,3,2,1,0:T(8,128)(2,1)}, u32[]{:S(2)}) copy-start(bf16[1,3,1,128,512]{4,3,2,1,0:T(8,128)(2,1)} %param.16) | copy-start | bytes 1179652
  60.0 350.4 %all-to-all-start.1 = ((bf16[96,128,512]{2,1,0:T(8,128)(2,1)}), bf16[96,128,512]{2,1,0:T(8,128)(2,1)}, u32[]{:S(2)}, u32[]{:S(2)}) async-start(bf16[96,128,512]{2,1,0:T(8,128)(2,1)} %bitcast.405), calls=%async_computation.1 | async-start | bytes 25165824 | tf_op jit(solution)/shard_map/all_to_all | solution.py:14
  71.1 6.0 copy-start.14
  75.7 409.7 %copy-start.68 = (pred[3,16]{1,0:T(4,128)(4,1)}, pred[3,16]{1,0:T(4,128)(4,1)S(1)}, u32[]{:S(2)}) copy-start(pred[3,16]{1,0:T(4,128)(4,1)S(1)} %get-tuple-element.61) | copy-start | bytes 148
  76.3 409.2 %copy-start.66 = (pred[3,16]{1,0:T(4,128)(4,1)}, pred[3,16]{1,0:T(4,128)(4,1)S(1)}, u32[]{:S(2)}) copy-start(pred[3,16]{1,0:T(4,128)(4,1)S(1)} %get-tuple-element.69) | copy-start | bytes 148
  76.4 38.9 %copy-start.45 = (s32[48]{0:T(128)}, s32[48]{0:T(128)S(1)}, u32[]{:S(2)}) copy-start(s32[48]{0:T(128)S(1)} %reshape.881) | copy-start | bytes 580
  76.4 38.9 %copy-start.43 = (s32[48]{0:T(128)}, s32[48]{0:T(128)S(1)}, u32[]{:S(2)}) copy-start(s32[48]{0:T(128)S(1)} %reshape.875) | copy-start | bytes 580
  94.8 387.7 %copy-start.37 = (bf16[3,128,128]{1,2,0:T(8,128)(2,1)}, bf16[3,128,128]{1,2,0:T(8,128)(2,1)S(1)}, u32[]{:S(2)}) copy-start(bf16[3,128,128]{1,2,0:T(8,128)(2,1)S(1)} %copy.969) | copy-start | bytes 294916
  106.4 8.1 copy-start.54
  107.2 6.5 copy-start.55
  471.1 2.7 copy-start.20
  482.6 2.8 copy-start.24
  484.2 2.9 copy-start.21
  484.2 3.4 copy-start.22
  484.2 3.8 copy-start.23
  488.1 4.9 copy-start.47
  492.9 6.3 copy-start.15
  492.9 6.3 copy-start.16
  492.9 6.2 copy-start.30
  492.9 6.2 copy-start.48
  505.2 4.0 copy-start.36
  505.3 4.0 copy-start.58
  515.8 3.3 copy-start.34
  515.8 3.3 copy-start.64
  519.0 28.2 %copy-start.4 = (bf16[3,2,128,16,128]{2,4,3,1,0:T(8,128)(2,1)}, bf16[3,2,128,16,128]{2,4,3,1,0:T(8,128)(2,1)S(1)}, u32[]{:S(2)}) copy-start(bf16[3,2,128,16,128]{2,4,3,1,0:T(8,128)(2,1)S(1)} %fusion.5) | copy-start | bytes 9437188
  524.5 2.9 copy-start.35
  524.5 2.9 copy-start.63
  527.4 36.5 %copy-start.5 = (bf16[3,2,128,16,128]{2,4,3,1,0:T(8,128)(2,1)}, bf16[3,2,128,16,128]{2,4,3,1,0:T(8,128)(2,1)S(1)}, u32[]{:S(2)}) copy-start(bf16[3,2,128,16,128]{2,4,3,1,0:T(8,128)(2,1)S(1)} %fusion.6) | copy-start | bytes 9437188
  530.3 6.5 slice-start
  533.8 3.0 copy-start.33
  533.8 3.0 copy-start.62
  533.8 3.0 slice-start.1
  536.8 23.9 %copy-start.6 = (bf16[3,2,128,16,128]{2,4,3,1,0:T(8,128)(2,1)}, bf16[3,2,128,16,128]{2,4,3,1,0:T(8,128)(2,1)S(1)}, u32[]{:S(2)}) copy-start(bf16[3,2,128,16,128]{2,4,3,1,0:T(8,128)(2,1)S(1)} %fusion.7) | copy-start | bytes 9437188
  542.4 4.8 copy-start.40
  547.3 10.4 %copy-start.7 = (bf16[3,2,128,16,128]{2,4,3,1,0:T(8,128)(2,1)}, bf16[3,2,128,16,128]{2,4,3,1,0:T(8,128)(2,1)S(1)}, u32[]{:S(2)}) copy-start(bf16[3,2,128,16,128]{2,4,3,1,0:T(8,128)(2,1)S(1)} %fusion.8) | copy-start | bytes 9437188
  552.7 3.0 copy-start.31
  599.1 3.6 copy-start.46
  642.4 7.9 copy-start.11
  644.7 49.7 %all-to-all-start.4 = ((bf16[8,128,512]{2,1,0:T(8,128)(2,1)}), bf16[8,128,512]{2,1,0:T(8,128)(2,1)}, u32[]{:S(2)}, u32[]{:S(2)}) async-start(bf16[8,128,512]{2,1,0:T(8,128)(2,1)} %pad_maximum_fusion.2), calls=%async_computation.4 | async-start | bytes 2097152 | tf_op jit(solution)/shard_map/all_to_all | solution.py:196
  692.1 7.4 copy-start.10
  694.4 52.2 %all-to-all-start.6 = ((bf16[8,128,512]{2,1,0:T(8,128)(2,1)}), bf16[8,128,512]{2,1,0:T(8,128)(2,1)}, u32[]{:S(2)}, u32[]{:S(2)}) async-start(bf16[8,128,512]{2,1,0:T(8,128)(2,1)} %pad_maximum_fusion.3), calls=%async_computation.6 | async-start | bytes 2097152 | tf_op jit(solution)/shard_map/all_to_all | solution.py:197
  746.6 9.7 copy-start.9
  746.6 102.9 %all-to-all-start.3 = ((bf16[32,128,512]{2,1,0:T(8,128)(2,1)}), bf16[32,128,512]{2,1,0:T(8,128)(2,1)}, u32[]{:S(2)}, u32[]{:S(2)}) async-start(bf16[32,128,512]{2,1,0:T(8,128)(2,1)} %pad_maximum_fusion), calls=%async_computation.3 | async-start | bytes 8388608 | tf_op jit(solution)/shard_map/all_to_all | solution.py:192
  803.5 57.0 %copy-start.57 = (bf16[3,2,64,128]{3,2,1,0:T(8,128)(2,1)S(1)}, bf16[3,2,64,128]{3,2,1,0:T(8,128)(2,1)}, u32[]{:S(2)}) copy-start(bf16[3,2,64,128]{3,2,1,0:T(8,128)(2,1)} %get-tuple-element.172) | copy-start | bytes 294916
  803.5 57.8 %copy-start.59 = (bf16[3,2,64,128]{3,2,1,0:T(8,128)(2,1)S(1)}, bf16[3,2,64,128]{3,2,1,0:T(8,128)(2,1)}, u32[]{:S(2)}) copy-start(bf16[3,2,64,128]{3,2,1,0:T(8,128)(2,1)} %get-tuple-element.174) | copy-start | bytes 294916
  803.5 58.5 %copy-start.60 = (bf16[3,2,64,128]{3,2,1,0:T(8,128)(2,1)S(1)}, bf16[3,2,64,128]{3,2,1,0:T(8,128)(2,1)}, u32[]{:S(2)}) copy-start(bf16[3,2,64,128]{3,2,1,0:T(8,128)(2,1)} %get-tuple-element.176) | copy-start | bytes 294916
  803.5 59.3 %copy-start.61 = (bf16[3,2,64,128]{3,2,1,0:T(8,128)(2,1)S(1)}, bf16[3,2,64,128]{3,2,1,0:T(8,128)(2,1)}, u32[]{:S(2)}) copy-start(bf16[3,2,64,128]{3,2,1,0:T(8,128)(2,1)} %get-tuple-element.178) | copy-start | bytes 294916
  803.5 60.0 %copy-start.3 = (bf16[3,16,128,128]{2,3,1,0:T(8,128)(2,1)S(1)}, bf16[3,16,128,128]{2,3,1,0:T(8,128)(2,1)}, u32[]{:S(2)}) copy-start(bf16[3,16,128,128]{2,3,1,0:T(8,128)(2,1)} %copy-done.2) | copy-start | bytes 4718596
  849.5 157.3 %all-to-all-start.5 = ((bf16[32,128,512]{2,1,0:T(8,128)(2,1)}), bf16[32,128,512]{2,1,0:T(8,128)(2,1)}, u32[]{:S(2)}, u32[]{:S(2)}) async-start(bf16[32,128,512]{2,1,0:T(8,128)(2,1)} %pad_maximum_fusion.1), calls=%async_computation.5 | async-start | bytes 8388608 | tf_op jit(solution)/shard_map/all_to_all | solution.py:193
  859.4 7.5 copy-start.1
  869.5 4.8 copy-start.8
  877.3 3.1 copy-start.42
  982.1 14.8 %copy-start.71 = (s32[8]{0:T(128)S(1)}, s32[8]{0:T(128)}, u32[]{:S(2)}) copy-start(s32[8]{0:T(128)} %copy-done.70) | copy-start | bytes 100
  1000.9 4.6 copy-start.49
  1006.8 4.7 copy-start.50
  1006.8 4.7 copy-start.51
  (18 other events, 29.1 us)
Sparse Core Ops, SparseCore 0:
  23.1 266.6 all-gather.2
